TPU v7x, 128 devices: a whole 4x4x4 slice. The times are simulated.
128 devices in a mesh: tm: 8 (over y, x_hi), agent: 16 (over z, x_lo, core).
Axes of the slice: x: 4 (x_hi: 2, x_lo: 2; x = x_hi * 2 + x_lo), y: 4, z: 4, core: 2. Of those that a mesh axis runs over, the one named last changes fastest.
Arguments:
- tokens: bfloat16 [32, 1024, 1024], P('tm', 'agent'), may hold values from -6 to 6
- conv_taps: float32 [5, 1024], replicated, may hold values from -3 to 3
- norm_first: float32 [1024], replicated, may hold values from 0.1 to 1.9
- norm_second: float32 [1024], replicated, may hold values from 0.1 to 1.9
- norm_third: float32 [1024], replicated, may hold values from 0.1 to 1.9
- w_in: bfloat16 [1024, 3072], replicated, may hold values from -0.1875 to 0.1875
- w_out: bfloat16 [3072, 1024], replicated, may hold values from -0.109375 to 0.109375
- w_query: bfloat16 [1024, 1024], replicated, may hold values from -16 to 16
- w_key: bfloat16 [1024, 1024], replicated, may hold values from -16 to 16
- w_value: bfloat16 [1024, 1024], replicated, may hold values from -0.1875 to 0.1875
- w_output: bfloat16 [1024, 1024], replicated, may hold values from -0.1875 to 0.1875
- agent_order: int32 [1024], P('agent'), may hold values from 0 to 1023, each once
- present_steps: int32 [1024], P('agent'), may hold values from 1 to 32
Outputs:
- result: bfloat16 [32, 1024, 1024], P('tm', 'agent')
Inputs may be any that keep to these rules, and one draw needn't show every extreme that they name: `agent_order`: each of 0 to 1023 appears once.
All inputs are finite; a program needn't handle non-finite values.
Results may differ from a plain program's by a relative error of at most 0.012.
Values may be sent and summed in bfloat16 or wider, within the bound.
A program may use at most 192 MiB of HBM per device.

v0:
```python
import jax
import jax.numpy as jnp
from jax import lax
from jax.sharding import PartitionSpec as P

HEADS = 16
EPS = 1e-05


def shifted(shard, axis, by):
    count = lax.axis_size(axis)
    pairs = [(i, i + by) for i in range(count) if 0 <= i + by < count]
    return lax.ppermute(shard, axis, pairs)


def normed_rows(rows, gain):
    values = rows.astype(jnp.float32)
    scale = lax.rsqrt(jnp.mean(values * values, axis=-1, keepdims=True) + EPS)
    return values * scale * gain


def make_absorb(query, own_order, steps, heads_here, project):
    step_count, agent_count, width = query.shape
    head_size = width // heads_here
    scale = head_size ** (-0.5)
    split_query = query.reshape(step_count, agent_count, heads_here, head_size)
    init = (
        jnp.full((step_count, heads_here, agent_count), -1e30, jnp.float32),
        jnp.zeros((step_count, heads_here, agent_count), jnp.float32),
        jnp.zeros((step_count, agent_count, heads_here, head_size), jnp.float32),
    )

    def absorb(carry, piece, start):
        best, total, summed = carry
        key_piece, value_piece, order_piece, present_piece = project(piece)
        count = key_piece.shape[1]
        key_piece = key_piece.reshape(step_count, count, heads_here, head_size)
        value_piece = value_piece.reshape(step_count, count, heads_here, head_size)
        scores = (
            jnp.einsum(
                "sahd,sbhd->shab", split_query, key_piece, preferred_element_type=jnp.float32
            )
            * scale
        )
        other_order = order_piece[0]
        earlier = other_order[None, None, :] < own_order[None, :, None]
        alive = steps[:, None, None] < present_piece[0][None, None, :]
        itself = other_order[None, None, :] == own_order[None, :, None]
        visible = (earlier & alive | itself)[:, None]
        masked = jnp.where(visible, scores, -1e30)
        fresh = jnp.maximum(best, jnp.max(masked, axis=-1))
        weights = jnp.where(visible, jnp.exp(masked - fresh[..., None]), 0.0).astype(jnp.bfloat16)
        total = jnp.sum(weights.astype(jnp.float32), axis=-1)
        part_sum = jnp.einsum(
            "shab,sbhd->sahd", weights, value_piece, preferred_element_type=jnp.float32
        )
        summed = part_sum
        return (fresh, total, summed)

    return (absorb, init)


def finish(carry, shape):
    best, total, summed = carry
    attended = summed / jnp.transpose(total, (0, 2, 1))[..., None]
    return attended.astype(jnp.bfloat16).reshape(shape)


def identity_piece(piece):
    return piece


def per_device(
    tokens,
    conv_taps,
    norm_first,
    norm_second,
    norm_third,
    w_in,
    w_out,
    w_query,
    w_key,
    w_value,
    w_output,
    agent_order,
    present_steps,
):
    step_count, agent_count, width = tokens.shape
    reach = conv_taps.shape[0] - 1
    earlier_steps = shifted(tokens, "tm", 1)
    extended = normed_rows(jnp.concatenate([earlier_steps, tokens], axis=0), norm_first)
    mixed = jnp.zeros((step_count, agent_count, width), jnp.float32)
    for lag in range(reach + 1):
        mixed = mixed + conv_taps[lag] * extended[reach - lag : reach - lag + step_count]
    first = (tokens.astype(jnp.float32) + mixed).astype(jnp.bfloat16)
    flat = first.reshape(step_count * agent_count, width)
    inner = normed_rows(flat, norm_second).astype(jnp.bfloat16)
    hidden = jax.nn.gelu(
        jnp.dot(inner, w_in, preferred_element_type=jnp.float32), approximate=False
    ).astype(jnp.bfloat16)
    second = (
        flat.astype(jnp.float32) + jnp.dot(hidden, w_out, preferred_element_type=jnp.float32)
    ).astype(jnp.bfloat16)
    attn_in = normed_rows(second, norm_third).astype(jnp.bfloat16)
    query = (
        jnp.dot(attn_in, w_query, preferred_element_type=jnp.float32)
        .astype(jnp.bfloat16)
        .reshape(step_count, agent_count, width)
    )
    order_rows = agent_order.reshape(1, agent_count)
    present_rows = present_steps.reshape(1, agent_count)
    keys = (
        jnp.dot(attn_in, w_key, preferred_element_type=jnp.float32)
        .astype(jnp.bfloat16)
        .reshape(step_count, agent_count, width)
    )
    values = (
        jnp.dot(attn_in, w_value, preferred_element_type=jnp.float32)
        .astype(jnp.bfloat16)
        .reshape(step_count, agent_count, width)
    )
    keys, values = (keys, values)
    query, keys, values = (
        lax.all_to_all(query, "tm", split_axis=2, concat_axis=0, tiled=True),
        lax.all_to_all(keys, "tm", split_axis=2, concat_axis=0, tiled=True),
        lax.all_to_all(values, "tm", split_axis=2, concat_axis=0, tiled=True),
    )
    steps = jnp.arange(query.shape[0], dtype=jnp.int32)
    heads_here = HEADS // lax.axis_size("tm")
    absorb, init = make_absorb(query, agent_order, steps, heads_here, identity_piece)
    carry = absorb(
        init,
        (
            lax.all_gather(keys, "agent", axis=1, tiled=True),
            lax.all_gather(values, "agent", axis=1, tiled=True),
            lax.all_gather(order_rows, "agent", axis=1, tiled=True),
            lax.all_gather(present_rows, "agent", axis=1, tiled=True),
        ),
        jnp.int32(0),
    )
    attended = finish(carry, query.shape)
    attended = lax.all_to_all(attended, "tm", split_axis=0, concat_axis=2, tiled=True)
    projected = jnp.dot(
        attended.reshape(step_count * agent_count, width),
        w_output,
        preferred_element_type=jnp.float32,
    )
    result = second.astype(jnp.float32) + projected
    return result.astype(jnp.bfloat16).reshape(step_count, agent_count, width)


def solution(mesh):
    in_specs = (
        P("tm", "agent", None),
        P(),
        P(),
        P(),
        P(),
        P(),
        P(),
        P(),
        P(),
        P(),
        P(),
        P("agent"),
        P("agent"),
    )
    out_specs = P("tm", "agent", None)
    return jax.shard_map(
        per_device, mesh=mesh, in_specs=in_specs, out_specs=out_specs, check_vma=False
    )
```

profile of v0, /device:TPU:0, one launch (start us, length us, event | category | flops | bytes accessed | tf_op | source)
XLA Modules:
  0.0 235.1 jit_solution(14129081017646608805)
XLA Ops:
  6.5 5.3 %collective-permute-start = (bf16[4,64,1024]{2,1,0:T(8,128)(2,1)}, bf16[4,64,1024]{2,1,0:T(8,128)(2,1)S(1)}, u32[]{:S(2)}, u32[]{:S(2)}) collective-permute-start(bf16[4,64,1024]{2,1,0:T(8,128)(2,1)} %param.13), channel_id=1, source_target_pairs={{0,16},{16,32},{32,48},{48,64},{64,80},{80,96},{96,112},{1,17},{17... | collective-permute-start | bytes 1572872 | tf_op jit(solution)/shard_map/ppermute | solution.py:13
  11.8 1.0 fusion.102
  12.8 10.5 %collective-permute-done = bf16[4,64,1024]{2,1,0:T(8,128)(2,1)S(1)} collective-permute-done((bf16[4,64,1024]{2,1,0:T(8,128)(2,1)}, bf16[4,64,1024]{2,1,0:T(8,128)(2,1)S(1)}, u32[]{:S(2)}, u32[]{:S(2)}) %collective-permute-start) | collective-permute-done | bytes 524320 | tf_op jit(solution)/shard_map/ppermute | solution.py:13
  23.3 1.3 fusion.11
  24.6 1.3 fusion.12
  26.0 0.6 multiply_reduce_fusion
  26.6 0.1 rsqrt.29
  26.7 0.2 fusion.63
  26.9 15.0 %fusion.53 = (f32[256]{0:T(256)S(1)}, bf16[256,1024]{1,0:T(8,128)(2,1)}) fusion(bf16[3072,1024]{1,0:T(8,128)(2,1)} %param.19, bf16[256,1024]{1,0:T(8,128)(2,1)S(1)} %fusion.63, bf16[1024,3072]{1,0:T(8,128)(2,1)} %param.18, bf16[256,1024]{1,0:T(8,128)(2,1)S(1)} %bitcast.69), kind=kOutput, calls=%fused_computation.70 | convolution fusion | flops 3273916160 | bytes 14156800 | tf_op jit(solution)/shard_map/dot_general | solution.py:102
  41.9 1.8 convolution_convert_fusion
  43.8 0.9 copy.31
  44.7 0.7 reshape.197
  45.4 18.3 %all_to_all.66 = bf16[8,2,16384]{2,1,0:T(2,128)(2,1)S(1)} all-to-all(bf16[8,2,16384]{2,1,0:T(2,128)(2,1)S(1)} %reshape.197), channel_id=1, replica_groups=mesh['tm'=8,'agent'=16] {'tm'}, dimensions={0} | all-to-all | bytes 1048576 | tf_op jit(solution)/shard_map/all_to_all | solution.py:125
  63.7 0.7 reshape.198
  64.3 1.4 copy.32
  65.7 0.0 all-gather.5.cloned.1.call-start
  65.8 2.4 %convolution_convert_fusion.2 = bf16[256,1024]{1,0:T(8,128)(2,1)S(1)} fusion(bf16[1024,1024]{1,0:T(8,128)(2,1)} %param.22, bf16[256,1024]{1,0:T(8,128)(2,1)S(1)} %copy-done.8, f32[1024]{0:T(1024)S(1)} %copy-done.5, f32[256]{0:T(256)S(1)} %add_rsqrt_fusion.2), kind=kOutput, calls=%fused_computation.68 | convolution fusion | flops 538181632 | bytes 3150848 | tf_op jit(solution)/shard_map/dot_general | solution.py:118
  68.2 0.7 copy.25
  68.9 0.7 reshape.195
  69.6 17.9 %all_to_all.67 = bf16[8,2,16384]{2,1,0:T(2,128)(2,1)S(1)} all-to-all(bf16[8,2,16384]{2,1,0:T(2,128)(2,1)S(1)} %reshape.195), channel_id=1, replica_groups=mesh['tm'=8,'agent'=16] {'tm'}, dimensions={0} | all-to-all | bytes 1048576 | tf_op jit(solution)/shard_map/all_to_all | solution.py:126
  87.5 0.7 reshape.196
  88.2 1.3 copy.26
  89.5 0.0 all-gather.5.cloned.1.call-update
  89.6 0.7 dynamic-slice
  91.0 0.2 dynamic-update-slice
  91.2 0.2 dynamic-update-slice.1
  91.4 14.2 %all-reduce.2 = (s32[1024]{0:T(1024)S(1)}, s32[1024]{0:T(1024)S(1)}) all-reduce(s32[1024]{0:T(1024)S(1)} %dynamic-update-slice, s32[1024]{0:T(1024)S(1)} %dynamic-update-slice.1), channel_id=2, replica_groups=mesh['tm'=8,'agent'=16] {'agent'}, use_global_device_ids=true, to_apply=%add | all-reduce | flops 2048 | bytes 16384
  105.7 0.1 broadcast_compare_fusion.1
  105.9 2.4 %convolution_convert_fusion.1 = bf16[256,1024]{1,0:T(8,128)(2,1)S(1)} fusion(bf16[1024,1024]{1,0:T(8,128)(2,1)} %param.20, bf16[256,1024]{1,0:T(8,128)(2,1)S(1)} %copy-done.8, f32[1024]{0:T(1024)S(1)} %copy-done.5, f32[256]{0:T(256)S(1)} %add_rsqrt_fusion.2), kind=kOutput, calls=%fused_computation.67 | convolution fusion | flops 538181632 | bytes 3150848 | tf_op jit(solution)/shard_map/dot_general | solution.py:106
  108.3 0.7 copy.28
  109.0 1.5 reshape.199
  110.5 4.4 %all-to-all-start.1 = ((bf16[8,2,16384]{2,1,0:T(2,128)(2,1)}), bf16[8,2,16384]{2,1,0:T(2,128)(2,1)}, u32[]{:S(2)}, u32[]{:S(2)}) async-start(bf16[8,2,16384]{2,1,0:T(2,128)(2,1)} %reshape.199), calls=%async_computation.1 | async-start | bytes 1048576 | tf_op jit(solution)/shard_map/all_to_all | solution.py:124
  114.9 1.4 and_or_fusion
  116.3 10.8 %all-to-all-done.1 = bf16[8,2,16384]{2,1,0:T(2,128)(2,1)} async-done(((bf16[8,2,16384]{2,1,0:T(2,128)(2,1)}), bf16[8,2,16384]{2,1,0:T(2,128)(2,1)}, u32[]{:S(2)}, u32[]{:S(2)}) %all-to-all-start.1) | async-done | bytes 524320 | tf_op jit(solution)/shard_map/all_to_all | solution.py:124
  127.1 2.7 %reshape.200 = bf16[1024,4,64]{2,1,0:T(4,128)(2,1)S(1)} reshape(bf16[8,2,16384]{2,1,0:T(2,128)(2,1)} %all-to-all-done.1) | data formatting | bytes 1048576
  129.8 1.2 copy.38
  131.0 2.4 %reshape.174 = bf16[32,64,2,64]{3,2,1,0:T(2,128)(2,1)S(1)} reshape(bf16[8,4,64,128]{3,2,1,0:T(8,128)(2,1)} %bitcast.70) | data formatting | bytes 1048576 | tf_op jit(solution)/shard_map/reshape | solution.py:26
  133.5 0.0 all-gather.7.cloned.1.call-done
  133.5 12.5 %copy.33 = bf16[32,1024,128]{1,2,0:T(8,128)(2,1)} copy(bf16[32,1024,128]{2,0,1:T(8,128)(2,1)} %all-gather.7.cloned.1.call-done) | data formatting | bytes 16777216 | tf_op jit(solution)/shard_map/all_gather | solution.py:134
  146.0 10.3 %fusion = (f32[32,2,64]{2,1,0:T(2,128)S(1)}, f32[32,2,64,1024]{3,2,1,0:T(8,128)}) fusion(pred[32,64,1024]{2,1,0:T(8,128)(4,1)S(1)} %and_or_fusion, bf16[32,1024,2,64]{1,3,2,0:T(8,128)(2,1)} %bitcast.61, bf16[32,64,2,64]{3,2,1,0:T(2,128)(2,1)S(1)} %reshape.174), kind=kOutput, calls=%fused_computation.3 | convolution fusion | flops 549449728 | bytes 27803648 | tf_op jit(solution)/shard_map/sahd,sbhd->shab/dot_general | solution.py:40
  156.3 9.0 %convert_reduce_fusion = f32[32,2,64]{2,1,0:T(2,128)S(1)} fusion(f32[32,2,64]{2,1,0:T(2,128)S(1)} %broadcast_maximum_fusion, f32[32,2,64,1024]{3,2,1,0:T(8,128)} %get-tuple-element.19, pred[32,64,1024]{2,1,0:T(8,128)(4,1)S(1)} %and_or_fusion), kind=kLoop, calls=%fused_computation | loop fusion | flops 29356032 | bytes 18907136 | tf_op jit(solution)/shard_map/reduce_sum | solution.py:53
  165.3 15.4 %all-gather.5.cloned.1.call-done = bf16[32,1024,128]{2,0,1:T(8,128)(2,1)} async-done(((bf16[32,64,128]{2,0,1:T(8,128)(2,1)}), bf16[32,1024,128]{2,0,1:T(8,128)(2,1)}) %all-gather.5.cloned.1.call-update) | async-done | bytes 8388624 | tf_op jit(solution)/shard_map/all_gather | solution.py:135
  180.7 12.2 %copy.27 = bf16[32,1024,128]{1,2,0:T(8,128)(2,1)} copy(bf16[32,1024,128]{2,0,1:T(8,128)(2,1)} %all-gather.5.cloned.1.call-done) | data formatting | bytes 16777216 | tf_op jit(solution)/shard_map/all_gather | solution.py:135
  192.9 11.7 %fusion.13 = bf16[32,64,2,64]{1,3,2,0:T(8,128)(2,1)} fusion(bf16[32,1024,2,64]{1,3,2,0:T(8,128)(2,1)} %bitcast.62, f32[32,64,2]{1,2,0:T(2,128)S(1)} %bitcast.79, f32[32,2,64,1024]{3,2,1,0:T(8,128)} %get-tuple-element.19, f32[32,2,64]{2,1,0:T(2,128)S(1)} %broadcast_maximum_fusion, pred[32,64,1024]{2,1,0:T(8,128)(4,1)S(1)} %and_or_fusion), kind=kOutput, calls=%fused_computation.29 | convolution fusion | flops 558366720 | bytes 27820032 | tf_op jit(solution)/shard_map/shab,sbhd->sahd/dot_general | solution.py:54
  204.6 1.7 copy.35
  206.3 18.5 %all_to_all.68 = bf16[32,64,128]{2,1,0:T(8,128)(2,1)S(1)} all-to-all(bf16[32,64,128]{2,1,0:T(8,128)(2,1)S(1)} %copy.35), channel_id=1, replica_groups=mesh['tm'=8,'agent'=16] {'tm'}, dimensions={0} | all-to-all | bytes 1048576 | tf_op jit(solution)/shard_map/all_to_all | solution.py:142
  224.8 0.3 copy.36
  225.2 3.1 %fusion.49 = bf16[256,1024]{1,0:T(8,128)(2,1)} fusion(bf16[1024,1024]{1,0:T(8,128)(2,1)} %param.23, bf16[256,1024]{1,0:T(8,128)(2,1)S(1)} %copy-done.9, bf16[32,8,8,128]{3,2,1,0:T(8,128)(2,1)S(1)} %bitcast.78), kind=kOutput, calls=%fused_computation.65 | convolution fusion | flops 537657344 | bytes 3670016 | tf_op jit(solution)/shard_map/dot_general | solution.py:143
  (29 shorter events, 0.1 us)
Async XLA Ops:
  6.5 35.4 %copy-start = (bf16[1024,1024]{1,0:T(8,128)(2,1)S(1)}, bf16[1024,1024]{1,0:T(8,128)(2,1)}, u32[]{:S(2)}) copy-start(bf16[1024,1024]{1,0:T(8,128)(2,1)} %param.21) | copy-start | bytes 6291460
  6.5 19.4 %copy-start.2 = (bf16[4,64,1024]{2,1,0:T(8,128)(2,1)S(1)}, bf16[4,64,1024]{2,1,0:T(8,128)(2,1)}, u32[]{:S(2)}) copy-start(bf16[4,64,1024]{2,1,0:T(8,128)(2,1)} %param.13) | copy-start | bytes 1572868
  6.5 127.0 %all-gather.7.cloned.1.call-start = ((), (), s32[]{:S(2)}) async-start(), calls=%async_computation.5 | async-start | bytes 8912896 | tf_op jit(solution)/shard_map/all_gather | solution.py:134
  6.5 16.8 %collective-permute-start = (bf16[4,64,1024]{2,1,0:T(8,128)(2,1)}, bf16[4,64,1024]{2,1,0:T(8,128)(2,1)S(1)}, u32[]{:S(2)}, u32[]{:S(2)}) collective-permute-start(bf16[4,64,1024]{2,1,0:T(8,128)(2,1)} %param.13), channel_id=1, source_target_pairs={{0,16},{16,32},{32,48},{48,64},{64,80},{80,96},{96,112},{1,17},{17... | collective-permute-start | bytes 1572872 | tf_op jit(solution)/shard_map/ppermute | solution.py:13
  26.0 0.7 copy-start.3
  26.9 15.1 %copy-start.5 = (f32[1024]{0:T(1024)S(1)}, f32[1024]{0:T(1024)}, u32[]{:S(2)}) copy-start(f32[1024]{0:T(1024)} %param.17) | copy-start | bytes 12292
  44.6 21.1 %copy-start.8 = (bf16[256,1024]{1,0:T(8,128)(2,1)S(1)}, bf16[256,1024]{1,0:T(8,128)(2,1)}, u32[]{:S(2)}) copy-start(bf16[256,1024]{1,0:T(8,128)(2,1)} %get-tuple-element.17) | copy-start | bytes 1572868
  65.7 114.9 %all-gather.5.cloned.1.call-start = ((), (), s32[]{:S(2)}) async-start(), calls=%async_computation.4 | async-start | bytes 8912896 | tf_op jit(solution)/shard_map/all_gather | solution.py:135
  68.9 20.7 %copy-start.7 = (u32[128]{0:T(128)S(1)}, u32[128]{0:T(128)}, u32[]{:S(2)}) copy-start(u32[128]{0:T(128)} %constant.80) | copy-start | bytes 1540
  68.9 22.1 %copy-start.4 = (s32[64]{0:T(128)S(1)}, s32[64]{0:T(128)}, u32[]{:S(2)}) copy-start(s32[64]{0:T(128)} %param.24) | copy-start | bytes 772
  68.9 22.3 %copy-start.6 = (s32[64]{0:T(128)S(1)}, s32[64]{0:T(128)}, u32[]{:S(2)}) copy-start(s32[64]{0:T(128)} %param.25) | copy-start | bytes 772
  110.5 16.5 %all-to-all-start.1 = ((bf16[8,2,16384]{2,1,0:T(2,128)(2,1)}), bf16[8,2,16384]{2,1,0:T(2,128)(2,1)}, u32[]{:S(2)}, u32[]{:S(2)}) async-start(bf16[8,2,16384]{2,1,0:T(2,128)(2,1)} %reshape.199), calls=%async_computation.1 | async-start | bytes 1048576 | tf_op jit(solution)/shard_map/all_to_all | solution.py:124
  204.6 20.6 %copy-start.9 = (bf16[256,1024]{1,0:T(8,128)(2,1)S(1)}, bf16[256,1024]{1,0:T(8,128)(2,1)}, u32[]{:S(2)}) copy-start(bf16[256,1024]{1,0:T(8,128)(2,1)} %get-tuple-element.17) | copy-start | bytes 1572868
  204.6 23.7 %copy-start.1 = (bf16[1024,1024]{1,0:T(8,128)(2,1)S(1)}, bf16[1024,1024]{1,0:T(8,128)(2,1)}, u32[]{:S(2)}) copy-start(bf16[1024,1024]{1,0:T(8,128)(2,1)} %param.21) | copy-start | bytes 6291460
Sparse Core Ops, SparseCore 0:
  65.8 53.2 all-gather.6
  120.8 59.7 all-gather.4
where the time goes:
time: 236 us; the launch traced here: 235 us
  blocking collectives  69 us (29%)
  matrix products  46.8 us (20%)
  local copies, waits for them, and re-layouts  44.6 us (19%)
  waiting for transfers between devices  36.7 us (16%)
  between operations  14.4 us (6%)
  other arithmetic  14 us (6%)
  starting transfers between devices  9.7 us (4%)
    all_to_all x1, blocking collectives, per_device(): lax.all_to_all(attended, 'tm', split_axis=0, concat_axis=2, tiled=True)  18.5 us
    all_to_all x1, blocking collectives, per_device(): lax.all_to_all(keys, 'tm', split_axis=2, concat_axis=0, tiled=True)  18.3 us
    all_to_all x1, blocking collectives, per_device(): lax.all_to_all(values, 'tm', split_axis=2, concat_axis=0, tiled=True)  17.9 us
    all_gather x1, waiting for transfers between devices, per_device(): lax.all_gather(values, 'agent', axis=1, tiled=True)  15.4 us
    dot_general x1, matrix products, per_device(): jnp.dot(hidden, w_out, preferred_element_type=jnp.float32)  15 us
    unnamed x1, blocking collectives  14.2 us
    all_gather x1, local copies, waits for them, and re-layouts, per_device(): lax.all_gather(keys, 'agent', axis=1, tiled=True)  12.5 us
    all_gather x1, local copies, waits for them, and re-layouts, per_device(): lax.all_gather(values, 'agent', axis=1, tiled=True)  12.2 us
  transfers between devices with their start and end apart: 4, of which 3 were waited for; matrix products, arithmetic and copies ran while one was open for 22% of the time, Pallas kernels for 0%

commit v1 on v0

--- a/solution.py
+++ b/solution.py
@@ -2,6 +2,7 @@
 import jax.numpy as jnp
 from jax import lax
 from jax.sharding import PartitionSpec as P
+from jax.lax import all_to_all, axis_size
 
 HEADS = 16
 EPS = 1e-05
@@ -139,7 +140,11 @@
         jnp.int32(0),
     )
     attended = finish(carry, query.shape)
-    attended = lax.all_to_all(attended, "tm", split_axis=0, concat_axis=2, tiled=True)
+    words_finish = lambda own_rows, along_dim, array_axis: jnp.concatenate(
+        all_to_all(jnp.stack(jnp.split(own_rows, axis_size("tm"), along_dim)), "tm", 0, 0),
+        array_axis,
+    )
+    attended = words_finish(attended, 0, 2)
     projected = jnp.dot(
         attended.reshape(step_count * agent_count, width),
         w_output,

time: 236 us -> 235 us (level)
    unnamed x31 -> x38, local copies, waits for them, and re-layouts: 8.13 us -> 8.15 us
where the time goes in v1:
time: 235 us; the launch traced here: 234 us
  blocking collectives  69.2 us (29%)
  matrix products  46 us (20%)
  local copies, waits for them, and re-layouts  43.9 us (19%)
  waiting for transfers between devices  36.8 us (16%)
  between operations  14.4 us (6%)
  other arithmetic  14.1 us (6%)
  starting transfers between devices  9.71 us (4%)
    all_to_all x1, blocking collectives, per_device(): all_to_all(jnp.stack(jnp.split(own_rows, axis_size('tm'), along_dim)), 't...  18.6 us
    all_to_all x1, blocking collectives, per_device(): lax.all_to_all(keys, 'tm', split_axis=2, concat_axis=0, tiled=True)  18.3 us
    all_to_all x1, blocking collectives, per_device(): lax.all_to_all(values, 'tm', split_axis=2, concat_axis=0, tiled=True)  17.9 us
    all_gather x1, waiting for transfers between devices, per_device(): lax.all_gather(values, 'agent', axis=1, tiled=True)  15.4 us
    dot_general x1, matrix products, per_device(): jnp.dot(hidden, w_out, preferred_element_type=jnp.float32)  15 us
    unnamed x1, blocking collectives  14.3 us
    all_gather x1, local copies, waits for them, and re-layouts, per_device(): lax.all_gather(keys, 'agent', axis=1, tiled=True)  12.5 us
    all_gather x1, local copies, waits for them, and re-layouts, per_device(): lax.all_gather(values, 'agent', axis=1, tiled=True)  12.2 us
  transfers between devices with their start and end apart: 4, of which 3 were waited for; matrix products, arithmetic and copies ran while one was open for 22% of the time, Pallas kernels for 0%

profile of v1, /device:TPU:0, one launch (start us, length us, event | category | flops | bytes accessed | tf_op | source)
XLA Modules:
  0.0 234.0 jit_solution(10452356320159106458)
XLA Ops:
  6.5 5.3 %collective-permute-start = (bf16[4,64,1024]{2,1,0:T(8,128)(2,1)}, bf16[4,64,1024]{2,1,0:T(8,128)(2,1)S(1)}, u32[]{:S(2)}, u32[]{:S(2)}) collective-permute-start(bf16[4,64,1024]{2,1,0:T(8,128)(2,1)} %param.13), channel_id=1, source_target_pairs={{0,16},{16,32},{32,48},{48,64},{64,80},{80,96},{96,112},{1,17},{17... | collective-permute-start | bytes 1572872 | tf_op jit(solution)/shard_map/ppermute | solution.py:14
  11.8 1.0 fusion.103
  12.8 10.5 %collective-permute-done = bf16[4,64,1024]{2,1,0:T(8,128)(2,1)S(1)} collective-permute-done((bf16[4,64,1024]{2,1,0:T(8,128)(2,1)}, bf16[4,64,1024]{2,1,0:T(8,128)(2,1)S(1)}, u32[]{:S(2)}, u32[]{:S(2)}) %collective-permute-start) | collective-permute-done | bytes 524320 | tf_op jit(solution)/shard_map/ppermute | solution.py:14
  23.3 1.3 fusion.11
  24.6 1.3 fusion.12
  26.0 0.6 multiply_reduce_fusion
  26.7 0.2 fusion.63
  26.9 15.0 %fusion.53 = (f32[256]{0:T(256)S(1)}, bf16[256,1024]{1,0:T(8,128)(2,1)}) fusion(bf16[3072,1024]{1,0:T(8,128)(2,1)} %param.19, bf16[256,1024]{1,0:T(8,128)(2,1)S(1)} %fusion.63, bf16[1024,3072]{1,0:T(8,128)(2,1)} %param.18, bf16[256,1024]{1,0:T(8,128)(2,1)S(1)} %bitcast.74), kind=kOutput, calls=%fused_computation.70 | convolution fusion | flops 3273916160 | bytes 14156800 | tf_op jit(solution)/shard_map/dot_general | solution.py:103
  41.9 1.8 convolution_convert_fusion
  43.8 0.9 copy.45
  44.7 0.7 reshape.209
  45.4 18.3 %all_to_all.56 = bf16[8,2,16384]{2,1,0:T(2,128)(2,1)S(1)} all-to-all(bf16[8,2,16384]{2,1,0:T(2,128)(2,1)S(1)} %reshape.209), channel_id=1, replica_groups=mesh['tm'=8,'agent'=16] {'tm'}, dimensions={0} | all-to-all | bytes 1048576 | tf_op jit(solution)/shard_map/all_to_all | solution.py:126
  63.7 0.7 reshape.210
  64.3 1.4 copy.46
  65.8 2.4 %convolution_convert_fusion.2 = bf16[256,1024]{1,0:T(8,128)(2,1)S(1)} fusion(bf16[1024,1024]{1,0:T(8,128)(2,1)} %param.22, bf16[256,1024]{1,0:T(8,128)(2,1)S(1)} %copy-done.8, f32[1024]{0:T(1024)S(1)} %copy-done.5, f32[256]{0:T(256)S(1)} %add_rsqrt_fusion.2), kind=kOutput, calls=%fused_computation.68 | convolution fusion | flops 538181632 | bytes 3150848 | tf_op jit(solution)/shard_map/dot_general | solution.py:119
  68.1 0.7 copy.39
  68.9 0.7 reshape.207
  69.6 17.9 %all_to_all.57 = bf16[8,2,16384]{2,1,0:T(2,128)(2,1)S(1)} all-to-all(bf16[8,2,16384]{2,1,0:T(2,128)(2,1)S(1)} %reshape.207), channel_id=1, replica_groups=mesh['tm'=8,'agent'=16] {'tm'}, dimensions={0} | all-to-all | bytes 1048576 | tf_op jit(solution)/shard_map/all_to_all | solution.py:127
  87.5 0.7 reshape.208
  88.2 1.4 copy.40
  89.6 0.6 dynamic-slice
  90.8 0.2 dynamic-update-slice
  91.0 0.2 dynamic-update-slice.1
  91.2 14.3 %all-reduce.2 = (s32[1024]{0:T(1024)S(1)}, s32[1024]{0:T(1024)S(1)}) all-reduce(s32[1024]{0:T(1024)S(1)} %dynamic-update-slice, s32[1024]{0:T(1024)S(1)} %dynamic-update-slice.1), channel_id=2, replica_groups=mesh['tm'=8,'agent'=16] {'agent'}, use_global_device_ids=true, to_apply=%add | all-reduce | flops 2048 | bytes 16384
  105.6 0.1 broadcast_compare_fusion.1
  105.7 2.4 %convolution_convert_fusion.1 = bf16[256,1024]{1,0:T(8,128)(2,1)S(1)} fusion(bf16[1024,1024]{1,0:T(8,128)(2,1)} %param.20, bf16[256,1024]{1,0:T(8,128)(2,1)S(1)} %copy-done.8, f32[1024]{0:T(1024)S(1)} %copy-done.5, f32[256]{0:T(256)S(1)} %add_rsqrt_fusion.2), kind=kOutput, calls=%fused_computation.67 | convolution fusion | flops 538181632 | bytes 3150848 | tf_op jit(solution)/shard_map/dot_general | solution.py:107
  108.1 0.7 copy.42
  108.9 1.5 reshape.211
  110.4 4.4 %all-to-all-start.1 = ((bf16[8,2,16384]{2,1,0:T(2,128)(2,1)}), bf16[8,2,16384]{2,1,0:T(2,128)(2,1)}, u32[]{:S(2)}, u32[]{:S(2)}) async-start(bf16[8,2,16384]{2,1,0:T(2,128)(2,1)} %reshape.211), calls=%async_computation.1 | async-start | bytes 1048576 | tf_op jit(solution)/shard_map/all_to_all | solution.py:125
  114.8 1.4 and_or_fusion
  116.2 10.9 %all-to-all-done.1 = bf16[8,2,16384]{2,1,0:T(2,128)(2,1)} async-done(((bf16[8,2,16384]{2,1,0:T(2,128)(2,1)}), bf16[8,2,16384]{2,1,0:T(2,128)(2,1)}, u32[]{:S(2)}, u32[]{:S(2)}) %all-to-all-start.1) | async-done | bytes 524320 | tf_op jit(solution)/shard_map/all_to_all | solution.py:125
  127.0 2.7 %reshape.212 = bf16[1024,4,64]{2,1,0:T(4,128)(2,1)S(1)} reshape(bf16[8,2,16384]{2,1,0:T(2,128)(2,1)} %all-to-all-done.1) | data formatting | bytes 1048576
  129.8 1.2 copy.59
  131.0 2.4 %reshape.187 = bf16[32,64,2,64]{3,2,1,0:T(2,128)(2,1)S(1)} reshape(bf16[8,4,64,128]{3,2,1,0:T(8,128)(2,1)} %bitcast.75) | data formatting | bytes 1048576 | tf_op jit(solution)/shard_map/reshape | solution.py:27
  133.5 12.5 %copy.47 = bf16[32,1024,128]{1,2,0:T(8,128)(2,1)} copy(bf16[32,1024,128]{2,0,1:T(8,128)(2,1)} %all-gather.7.cloned.1.call-done) | data formatting | bytes 16777216 | tf_op jit(solution)/shard_map/all_gather | solution.py:135
  145.9 10.3 %fusion = (f32[32,2,64]{2,1,0:T(2,128)S(1)}, f32[32,2,64,1024]{3,2,1,0:T(8,128)}) fusion(pred[32,64,1024]{2,1,0:T(8,128)(4,1)S(1)} %and_or_fusion, bf16[32,1024,2,64]{1,3,2,0:T(8,128)(2,1)} %bitcast.66, bf16[32,64,2,64]{3,2,1,0:T(2,128)(2,1)S(1)} %reshape.187), kind=kOutput, calls=%fused_computation.3 | convolution fusion | flops 549449728 | bytes 27803648 | tf_op jit(solution)/shard_map/sahd,sbhd->shab/dot_general | solution.py:41
  156.3 9.0 %convert_reduce_fusion = f32[32,2,64]{2,1,0:T(2,128)S(1)} fusion(f32[32,2,64]{2,1,0:T(2,128)S(1)} %broadcast_maximum_fusion, f32[32,2,64,1024]{3,2,1,0:T(8,128)} %get-tuple-element.27, pred[32,64,1024]{2,1,0:T(8,128)(4,1)S(1)} %and_or_fusion), kind=kLoop, calls=%fused_computation | loop fusion | flops 29356032 | bytes 18907136 | tf_op jit(solution)/shard_map/reduce_sum | solution.py:54
  165.3 15.4 %all-gather.5.cloned.1.call-done = bf16[32,1024,128]{2,0,1:T(8,128)(2,1)} async-done(((bf16[32,64,128]{2,0,1:T(8,128)(2,1)}), bf16[32,1024,128]{2,0,1:T(8,128)(2,1)}) %all-gather.5.cloned.1.call-update) | async-done | bytes 8388624 | tf_op jit(solution)/shard_map/all_gather | solution.py:136
  180.7 12.2 %copy.41 = bf16[32,1024,128]{1,2,0:T(8,128)(2,1)} copy(bf16[32,1024,128]{2,0,1:T(8,128)(2,1)} %all-gather.5.cloned.1.call-done) | data formatting | bytes 16777216 | tf_op jit(solution)/shard_map/all_gather | solution.py:136
  192.9 11.0 %fusion.13 = bf16[32,64,2,64]{1,3,2,0:T(8,128)(2,1)S(1)} fusion(bf16[32,1024,2,64]{1,3,2,0:T(8,128)(2,1)} %bitcast.67, f32[32,64,2]{1,2,0:T(2,128)S(1)} %bitcast.91, f32[32,2,64,1024]{3,2,1,0:T(8,128)} %get-tuple-element.27, f32[32,2,64]{2,1,0:T(2,128)S(1)} %broadcast_maximum_fusion, pred[32,64,1024]{2,1,0:T(8,128)(4,1)S(1)} %and_or_fusion), kind=kOutput, calls=%fused_computation.29 | convolution fusion | flops 558366720 | bytes 27820032 | tf_op jit(solution)/shard_map/shab,sbhd->sahd/dot_general | solution.py:55
  204.0 0.1 copy.49
  204.3 0.1 copy.51
  204.4 0.1 copy.52
  204.6 0.1 copy.54
  204.7 0.1 copy.55
  205.1 18.6 %all_to_all.58 = bf16[8,4,64,128]{3,2,1,0:T(8,128)(2,1)S(1)} all-to-all(bf16[8,4,64,128]{3,2,1,0:T(8,128)(2,1)S(1)} %constant_dynamic-update-slice_fusion), channel_id=1, replica_groups=mesh['tm'=8,'agent'=16] {'tm'}, dimensions={0} | all-to-all | bytes 1048576 | tf_op jit(solution)/shard_map/all_to_all | solution.py:144
  223.7 0.3 copy.57
  224.1 3.1 %fusion.49 = bf16[256,1024]{1,0:T(8,128)(2,1)} fusion(bf16[1024,1024]{1,0:T(8,128)(2,1)} %param.23, bf16[256,1024]{1,0:T(8,128)(2,1)S(1)} %copy-done.9, bf16[32,8,8,128]{3,2,1,0:T(8,128)(2,1)S(1)} %bitcast.90), kind=kOutput, calls=%fused_computation.65 | convolution fusion | flops 537657344 | bytes 3670016 | tf_op jit(solution)/shard_map/dot_general | solution.py:148
  (45 shorter events, 0.8 us)
Async XLA Ops:
  6.5 35.4 %copy-start = (bf16[1024,1024]{1,0:T(8,128)(2,1)S(1)}, bf16[1024,1024]{1,0:T(8,128)(2,1)}, u32[]{:S(2)}) copy-start(bf16[1024,1024]{1,0:T(8,128)(2,1)} %param.21) | copy-start | bytes 6291460
  6.5 19.4 %copy-start.2 = (bf16[4,64,1024]{2,1,0:T(8,128)(2,1)S(1)}, bf16[4,64,1024]{2,1,0:T(8,128)(2,1)}, u32[]{:S(2)}) copy-start(bf16[4,64,1024]{2,1,0:T(8,128)(2,1)} %param.13) | copy-start | bytes 1572868
  6.5 126.9 %all-gather.7.cloned.1.call-start = ((), (), s32[]{:S(2)}) async-start(), calls=%async_computation.5 | async-start | bytes 8912896 | tf_op jit(solution)/shard_map/all_gather | solution.py:135
  6.5 16.8 %collective-permute-start = (bf16[4,64,1024]{2,1,0:T(8,128)(2,1)}, bf16[4,64,1024]{2,1,0:T(8,128)(2,1)S(1)}, u32[]{:S(2)}, u32[]{:S(2)}) collective-permute-start(bf16[4,64,1024]{2,1,0:T(8,128)(2,1)} %param.13), channel_id=1, source_target_pairs={{0,16},{16,32},{32,48},{48,64},{64,80},{80,96},{96,112},{1,17},{17... | collective-permute-start | bytes 1572872 | tf_op jit(solution)/shard_map/ppermute | solution.py:14
  26.0 0.7 copy-start.3
  26.9 15.1 %copy-start.5 = (f32[1024]{0:T(1024)S(1)}, f32[1024]{0:T(1024)}, u32[]{:S(2)}) copy-start(f32[1024]{0:T(1024)} %param.17) | copy-start | bytes 12292
  44.6 21.1 %copy-start.8 = (bf16[256,1024]{1,0:T(8,128)(2,1)S(1)}, bf16[256,1024]{1,0:T(8,128)(2,1)}, u32[]{:S(2)}) copy-start(bf16[256,1024]{1,0:T(8,128)(2,1)} %get-tuple-element.25) | copy-start | bytes 1572868
  65.7 115.0 %all-gather.5.cloned.1.call-start = ((), (), s32[]{:S(2)}) async-start(), calls=%async_computation.4 | async-start | bytes 8912896 | tf_op jit(solution)/shard_map/all_gather | solution.py:136
  68.9 20.7 %copy-start.7 = (u32[128]{0:T(128)S(1)}, u32[128]{0:T(128)}, u32[]{:S(2)}) copy-start(u32[128]{0:T(128)} %constant.80) | copy-start | bytes 1540
  68.9 21.9 %copy-start.4 = (s32[64]{0:T(128)S(1)}, s32[64]{0:T(128)}, u32[]{:S(2)}) copy-start(s32[64]{0:T(128)} %param.24) | copy-start | bytes 772
  68.9 22.1 %copy-start.6 = (s32[64]{0:T(128)S(1)}, s32[64]{0:T(128)}, u32[]{:S(2)}) copy-start(s32[64]{0:T(128)} %param.25) | copy-start | bytes 772
  110.4 16.7 %all-to-all-start.1 = ((bf16[8,2,16384]{2,1,0:T(2,128)(2,1)}), bf16[8,2,16384]{2,1,0:T(2,128)(2,1)}, u32[]{:S(2)}, u32[]{:S(2)}) async-start(bf16[8,2,16384]{2,1,0:T(2,128)(2,1)} %reshape.211), calls=%async_computation.1 | async-start | bytes 1048576 | tf_op jit(solution)/shard_map/all_to_all | solution.py:125
  203.9 20.2 %copy-start.9 = (bf16[256,1024]{1,0:T(8,128)(2,1)S(1)}, bf16[256,1024]{1,0:T(8,128)(2,1)}, u32[]{:S(2)}) copy-start(bf16[256,1024]{1,0:T(8,128)(2,1)} %get-tuple-element.25) | copy-start | bytes 1572868
  205.0 22.2 %copy-start.1 = (bf16[1024,1024]{1,0:T(8,128)(2,1)S(1)}, bf16[1024,1024]{1,0:T(8,128)(2,1)}, u32[]{:S(2)}) copy-start(bf16[1024,1024]{1,0:T(8,128)(2,1)} %param.21) | copy-start | bytes 6291460
Sparse Core Ops, SparseCore 0:
  65.8 53.3 all-gather.6
  120.9 59.7 all-gather.4
